TPU v7x, 256 devices: a whole 4x4x8 slice. The times are simulated.
256 devices in a mesh: seq: 64 (over x, z, core), tp: 4 (over y).
Axes of the slice: x: 4, y: 4, z: 8, core: 2. Of those that a mesh axis runs over, the one named last changes fastest.
Arguments:
- hidden_in: bfloat16 [16384, 1536], P('seq', 'tp'), may hold values from -6 to 6
- w_in_gate: float32 [1536, 3072], P('seq', 'tp'), may hold values from -0.15625 to 0.15625
- w_in_value: float32 [1536, 3072], P('seq', 'tp'), may hold values from -0.15625 to 0.15625
- w_in_shared: float32 [1536, 256], P('seq'), may hold values from -0.15625 to 0.15625
- w_in_step: float32 [1536, 48], P('seq', 'tp'), may hold values from -0.15625 to 0.15625
- conv_value: float32 [4, 3072], P(None, 'tp'), may hold values from -3 to 3
- conv_shared: float32 [4, 256], replicated, may hold values from -3 to 3
- dt_bias: float32 [48], P('tp'), may hold values from -4 to -2
- a_log: float32 [48], P('tp'), may hold values from -8 to 0
- skip_gain: float32 [48], P('tp'), may hold values from 0.6 to 4.8
- norm_gain: float32 [3072], P('tp'), may hold values from 0.1 to 1.9
- w_out: float32 [3072, 1536], P('tp', 'seq'), may hold values from -0.109375 to 0.109375
- prompt_lengths: int32 [8], replicated, may hold values from 1 to 8192, 16384 in all
- row_blocks: int32 [64], replicated, may hold values from 0 to 63, each once
Outputs:
- mixed_out: bfloat16 [16384, 1536], P('seq', 'tp')
Inputs may be any that keep to these rules, and one draw needn't show every extreme that they name: `prompt_lengths`: 8 lengths that sum to 16384, the longest exactly 8192. `row_blocks`: a permutation of the row blocks.
All inputs are finite; a program needn't handle non-finite values.
Results may differ from a plain program's by a relative error of at most 0.02.
Values may be sent and summed in bfloat16 or wider, within the bound.
No kernel may reach another device: no remote copies, remote signals or barrier semaphores. Data moves between devices by JAX's collectives and lax.ppermute only.
A program may use at most 128 MiB of HBM per device.

v0:
```python
import jax
import jax.numpy as jnp
from jax import lax
from jax.sharding import PartitionSpec as P

EPSILON = 1e-05
HIGHEST_PREC = lax.Precision.HIGHEST


def passed_along(block, axis, distance):
    devices = range(lax.axis_size(axis))
    route = [(i - distance, i) for i in devices if i - distance in devices]
    return lax.ppermute(block, axis, route)


def prefix_2(x, axis, combine, identity):
    count, here = (lax.axis_size(axis), lax.axis_index(axis))
    everything = jax.tree.map(
        lambda part, kind: lax.all_gather(part.astype(kind), axis), x, (jnp.bfloat16, jnp.bfloat16)
    )
    start = jax.tree.map(
        lambda part, zero: jnp.broadcast_to(jnp.asarray(zero, part.dtype), part.shape), x, identity
    )

    def turn(k, before):
        reached = k < here
        new = combine(
            before, jax.tree.map(lambda part, own: part[k].astype(own.dtype), everything, x)
        )
        return jax.tree.map(lambda a, b: jnp.where(reached, a, b), new, before)

    return lax.fori_loop(0, count, turn, start)


def segment_of(positions, doc_ends):
    return jnp.sum((positions[:, None] >= doc_ends[None, :]).astype(jnp.int32), axis=1)


def span_parts(values, b_half, c_half, steps_dt, decay_rates, segments, prev_seg):
    length = values.shape[0]
    b_rows = b_half.astype(jnp.float32)
    cumulative = jnp.cumsum(-steps_dt * decay_rates[None, :], axis=0)
    places = jnp.arange(length)
    causal = (places[:, None] >= places[None, :]) & (segments[:, None] == segments[None, :])
    gaps_log = jnp.where(causal[:, :, None], cumulative[:, None, :] - cumulative[None, :, :], 0.0)
    decays_in = jnp.where(causal[:, :, None], jnp.exp(gaps_log), 0.0)
    scores = jnp.dot(c_half, b_half.T, preferred_element_type=jnp.float32)
    weights = scores[:, :, None] * decays_in * steps_dt[None, :, :]
    intra_part = jnp.einsum("ijh,jhp->ihp", weights, values, precision=HIGHEST_PREC)
    carry_in = jnp.where((segments == prev_seg)[:, None], jnp.exp(cumulative), 0.0)
    tail_weight = (
        jnp.where(
            (segments == segments[-1])[:, None], jnp.exp(cumulative[-1][None, :] - cumulative), 0.0
        )
        * steps_dt
    )
    fresh_state = jnp.einsum("jh,jhp,jn->hpn", tail_weight, values, b_rows, precision=HIGHEST_PREC)
    keep_factor = jnp.where(segments[-1] == prev_seg, jnp.exp(cumulative[-1]), 0.0)
    return (intra_part, carry_in, fresh_state, keep_factor)


def combine(earlier, later):
    return (earlier[0] * later[0], later[0][:, None, None] * earlier[1] + later[1])


def on_device(
    hidden_in,
    w_in_gate,
    w_in_value,
    w_in_shared,
    w_in_step,
    conv_value,
    conv_shared,
    dt_bias,
    a_log,
    skip_gain,
    norm_gain,
    w_out,
    prompt_lengths,
    row_blocks,
):
    seq_count = lax.axis_size("seq")
    tokens_here = hidden_in.shape[0]
    edge_count = conv_value.shape[0] - 1
    gathered = lax.all_gather(hidden_in, "tp", axis=1, tiled=True)
    row_count = gathered.shape[0]
    model_width = gathered.shape[1]
    permuted = jnp.take(
        gathered.reshape(row_count, seq_count, model_width // seq_count), row_blocks, axis=1
    ).reshape(row_count, model_width)
    stored = (
        w_in_gate.astype(jnp.bfloat16),
        w_in_value.astype(jnp.bfloat16),
        w_in_shared.astype(jnp.bfloat16),
        w_in_step.astype(jnp.bfloat16),
    )
    pieces = (
        lax.all_gather(stored[0], "seq", axis=0, tiled=True),
        lax.all_gather(stored[1], "seq", axis=0, tiled=True),
        lax.all_gather(stored[2], "seq", axis=0, tiled=True),
        lax.all_gather(stored[3], "seq", axis=0, tiled=True),
    )
    projected = tuple(
        (
            jnp.dot(permuted, weight_piece, preferred_element_type=jnp.float32)
            for weight_piece in pieces
        )
    )
    gate_all, value_all, shared_all, raw_all = [result.astype(jnp.bfloat16) for result in projected]
    mixed_in = jnp.concatenate([value_all, shared_all], axis=1)
    edge_mix = passed_along(mixed_in[tokens_here - edge_count :], "seq", 1)
    doc_ends = jnp.cumsum(prompt_lengths)
    first_pos = lax.axis_index("seq") * tokens_here
    positions = first_pos + jnp.arange(tokens_here, dtype=jnp.int32)
    edge_positions = first_pos - edge_count + jnp.arange(edge_count, dtype=jnp.int32)
    segments = segment_of(positions, doc_ends)
    ext_segments = jnp.concatenate([segment_of(edge_positions, doc_ends), segments])
    ext_rows = jnp.concatenate([edge_mix, mixed_in], axis=0)
    kernel = jnp.concatenate([conv_value, conv_shared], axis=1)
    conv_sum = jnp.zeros(mixed_in.shape, jnp.float32)
    for tap_index in range(edge_count + 1):
        same_doc = (ext_segments[tap_index : tap_index + tokens_here] == segments)[:, None]
        conv_sum = conv_sum + jnp.where(
            same_doc,
            kernel[tap_index][None, :]
            * ext_rows[tap_index : tap_index + tokens_here].astype(jnp.float32),
            0.0,
        )
    convolved = jax.nn.silu(conv_sum).astype(jnp.bfloat16)
    local_inner = conv_value.shape[1]
    local_heads = dt_bias.shape[0]
    head_dim = local_inner // local_heads
    state_size = conv_shared.shape[1] // 2
    values = (
        convolved[:, :local_inner].astype(jnp.float32).reshape(tokens_here, local_heads, head_dim)
    )
    b_half = convolved[:, local_inner : local_inner + state_size]
    c_half = convolved[:, local_inner + state_size :]
    c_rows = c_half.astype(jnp.float32)
    steps_dt = jax.nn.softplus(raw_all.astype(jnp.float32) + dt_bias[None, :])
    decay_rates = jnp.exp(a_log)
    prev_first = segment_of(jnp.reshape(first_pos - 1, (1,)), doc_ends)[0]
    device_keep = jnp.ones((local_heads,), jnp.float32)
    device_state = jnp.zeros((local_heads, head_dim, state_size), jnp.float32)
    parts = span_parts(values, b_half, c_half, steps_dt, decay_rates, segments, prev_first)
    device_keep = parts[3] * device_keep
    device_state = parts[3][:, None, None] * device_state + parts[2]
    identity = (jnp.ones_like(device_keep), jnp.zeros_like(device_state))
    prefix = prefix_2((device_keep, device_state), "seq", combine, identity)
    carried = prefix[1]
    intra_part, carry_in, fresh_state, keep_factor = parts
    inter_part = (
        jnp.einsum("in,hpn->ihp", c_rows, carried, precision=HIGHEST_PREC) * carry_in[:, :, None]
    )
    outputs = intra_part + inter_part
    mixed_heads = outputs + skip_gain[None, :, None] * values
    gated = mixed_heads.reshape(tokens_here, local_inner) * jax.nn.silu(
        gate_all.astype(jnp.float32)
    )
    squares = jnp.sum(gated * gated, axis=1)
    square_total = lax.psum(squares, "tp")
    mean_square = square_total / (local_inner * lax.axis_size("tp"))
    normed = (gated * lax.rsqrt(mean_square + EPSILON)[:, None] * norm_gain[None, :]).astype(
        jnp.bfloat16
    )
    out_weight = w_out.astype(jnp.bfloat16)
    partial_terms = jnp.dot(
        normed,
        lax.all_gather(out_weight, "seq", axis=1, tiled=True),
        preferred_element_type=jnp.float32,
    )
    return lax.psum_scatter(
        partial_terms.astype(jnp.bfloat16), "tp", scatter_dimension=1, tiled=True
    )


def solution(mesh):
    return jax.shard_map(
        on_device,
        mesh=mesh,
        in_specs=(
            P("seq", "tp"),
            P("seq", "tp"),
            P("seq", "tp"),
            P("seq", None),
            P("seq", "tp"),
            P(None, "tp"),
            P(),
            P("tp"),
            P("tp"),
            P("tp"),
            P("tp"),
            P("tp", "seq"),
            P(),
            P(),
        ),
        out_specs=P("seq", "tp"),
        check_vma=False,
    )
```

profile of v0, /device:TPU:2, one launch (start us, length us, event | category | flops | bytes accessed | tf_op | source)
XLA Modules:
  0.0 420.0 jit_solution(3729731392679539498)
XLA Ops:
  6.5 1.5 convert_element_type.112
  13.0 46.7 %all-gather.1 = bf16[64,24,12]{1,2,0:T(8,128)(2,1)S(1)} all-gather(bf16[1,24,12]{1,2,0:T(8,128)(2,1)S(1)} %convert_bitcast_fusion), channel_id=1, replica_groups=mesh['seq'=64,'tp'=4] {'seq'}, dimensions={0}, use_global_device_ids=true | all-gather | bytes 37440 | tf_op jit(solution)/shard_map/all_gather | solution.py:101
  61.4 14.2 %all_gather.28 = bf16[256,1536]{0,1:T(8,128)(2,1)S(1)} all-gather(bf16[256,384]{0,1:T(8,128)(2,1)S(1)} %copy.39), channel_id=1, replica_groups=mesh['seq'=64,'tp'=4] {'tp'}, dimensions={1}, use_global_device_ids=true | all-gather | bytes 983040 | tf_op jit(solution)/shard_map/all_gather | solution.py:85
  80.0 48.3 %all_gather.30 = bf16[1536,256]{1,0:T(8,128)(2,1)S(1)} all-gather(bf16[24,256]{1,0:T(8,128)(2,1)S(1)} %convert_element_type.114), channel_id=1, replica_groups=mesh['seq'=64,'tp'=4] {'seq'}, dimensions={0}, use_global_device_ids=true | all-gather | bytes 798720 | tf_op jit(solution)/shard_map/all_gather | solution.py:100
  128.3 1.3 broadcast_compare_fusion
  130.1 2.5 convolution_convert_fusion.2
  132.6 2.3 collective-permute-start
  134.9 4.8 %collective-permute-done = bf16[3,1024]{1,0:T(4,128)(2,1)S(1)} collective-permute-done((bf16[3,1024]{1,0:T(4,128)(2,1)S(1)}, bf16[3,1024]{1,0:T(4,128)(2,1)S(1)}, u32[]{:S(2)}, u32[]{:S(2)}) %collective-permute-start) | collective-permute-done | bytes 6176 | tf_op jit(solution)/shard_map/ppermute | solution.py:13
  140.9 1.2 fusion.20
  143.9 38.1 %all-gather.2 = bf16[64,1,12]{2,1,0:T(2,128)(2,1)S(1)} all-gather(bf16[1,1,12]{2,1,0:T(2,128)(2,1)S(1)} %bitcast.96), channel_id=1, replica_groups=mesh['seq'=64,'tp'=4] {'seq'}, dimensions={0}, use_global_device_ids=true | all-gather | bytes 1560 | tf_op jit(solution)/shard_map/all_gather | solution.py:19
  182.2 3.6 fusion.14
  185.8 43.4 %all-gather.14.cloned.1.call-done = bf16[768,64,128]{2,1,0:T(8,128)(2,1)} async-done(((bf16[12,64,128]{2,1,0:T(8,128)(2,1)}), bf16[768,64,128]{2,1,0:T(8,128)(2,1)}) %all-gather.14.cloned.1.call-update) | async-done | bytes 12582928 | tf_op jit(solution)/shard_map/all_gather | solution.py:19
  229.1 70.1 %while.14 = (s32[]{:T(128)}, f32[12,64,128]{2,1,0:T(8,128)S(1)}, s32[]{:T(128)}, bf16[64,12]{1,0:T(8,128)(2,1)S(1)}, bf16[64,12,64,128]{3,2,1,0:T(8,128)(2,1)}, /*index=5*/s32[]{:T(128)}, s32[]{:T(128)}) while((s32[]{:T(128)}, f32[12,64,128]{2,1,0:T(8,128)S(1)}, s32[]{:T(128)}, bf16[64,12]{1,0:T(8,128)(2,1)S(1)}, ...), condition=%wide.region_7.8_spmd.clone, body=%wide.region_6.7_spmd.clone.sunk | while | flops 491536 | bytes 983265 | solution.py:32
  278.4 1.1 fusion.58
  283.9 1.1 fusion.58
  299.3 1.6 fusion.18
  301.2 5.5 %all-gather.10.cloned.1.call-done = bf16[1536,768]{1,0:T(8,128)(2,1)} async-done(((bf16[24,768]{1,0:T(8,128)(2,1)}), bf16[1536,768]{1,0:T(8,128)(2,1)}) %all-gather.10.cloned.1.call-update) | async-done | bytes 2359312 | tf_op jit(solution)/shard_map/all_gather | solution.py:98
  306.7 2.7 multiply_reduce_fusion
  309.4 10.5 %psum.7 = f32[256]{0:T(256)S(1)} all-reduce(f32[256]{0:T(256)S(1)} %get-tuple-element.160), channel_id=1, replica_groups=mesh['seq'=64,'tp'=4] {'tp'}, use_global_device_ids=true, to_apply=%region_9.10 | all-reduce | flops 256 | bytes 2048 | tf_op jit(solution)/shard_map/psum | solution.py:161
  319.8 64.6 %all-gather.12.cloned.1.call-done = bf16[768,1536]{0,1:T(8,128)(2,1)} async-done(((bf16[768,24]{0,1:T(8,128)(2,1)}), bf16[768,1536]{0,1:T(8,128)(2,1)}) %all-gather.12.cloned.1.call-update) | async-done | bytes 2359312 | tf_op jit(solution)/shard_map/all_gather | solution.py:169
  384.4 2.5 convolution_convert_fusion
  386.9 1.2 copy.50
  388.1 23.7 %reduce-scatter.4.cloned.1.call-done = bf16[384,256]{1,0:T(8,128)(2,1)} async-done(((bf16[1536,256]{1,0:T(8,128)(2,1)}), bf16[384,256]{1,0:T(8,128)(2,1)}) %reduce-scatter.4.cloned.1.call-update) | async-done | bytes 196624
  411.8 1.7 copy.51
  (204 shorter events, 79.5 us)
Async XLA Ops:
  6.5 123.6 %all-gather.8.cloned.1.call-start = ((), (), s32[]{:S(2)}) async-start(), calls=%async_computation.1 | async-start | bytes 2396160 | tf_op jit(solution)/shard_map/all_gather | solution.py:99
  8.1 221.1 %all-gather.14.cloned.1.call-start = ((), (), s32[]{:S(2)}) async-start(), calls=%async_computation.4 | async-start | bytes 12779520 | tf_op jit(solution)/shard_map/all_gather | solution.py:19
  75.6 0.9 copy-start.5
  76.2 3.6 copy-start.2
  76.2 3.6 copy-start.4
  132.6 7.1 %collective-permute-start = (bf16[3,1024]{1,0:T(4,128)(2,1)S(1)}, bf16[3,1024]{1,0:T(4,128)(2,1)S(1)}, u32[]{:S(2)}, u32[]{:S(2)}) collective-permute-start(bf16[3,1024]{1,0:T(4,128)(2,1)S(1)} %fusion.40), channel_id=1, source_target_pairs={{0,4},{4,8},{8,12},{12,16},{16,20},{20,24},{24,28},{28,32},{32,36}... | collective-permute-start | bytes 18440 | tf_op jit(solution)/shard_map/ppermute | solution.py:13
  139.9 2.3 copy-start
  139.9 3.1 copy-start.1
  142.2 164.5 %all-gather.10.cloned.1.call-start = ((), (), s32[]{:S(2)}) async-start(), calls=%async_computation.2 | async-start | bytes 2396160 | tf_op jit(solution)/shard_map/all_gather | solution.py:98
  142.9 241.5 %all-gather.12.cloned.1.call-start = ((), (), s32[]{:S(2)}) async-start(), calls=%async_computation.3 | async-start | bytes 2396160 | tf_op jit(solution)/shard_map/all_gather | solution.py:169
  143.6 268.2 %reduce-scatter.4.cloned.1.call-start = ((), (), s32[]{:S(2)}) async-start(), calls=%async_computation.5 | async-start | bytes 983040
  229.1 70.1 %copy-start.6 = (f32[12]{0:T(128)S(1)}, f32[12]{0:T(128)}, u32[]{:S(2)}) copy-start(f32[12]{0:T(128)} %param.25) | copy-start | bytes 148
  301.2 83.2 %copy-start.3 = (f32[768]{0:T(1024)S(1)}, f32[768]{0:T(1024)}, u32[]{:S(2)}) copy-start(f32[768]{0:T(1024)} %param.26) | copy-start | bytes 9220
Sparse Core Ops, SparseCore 0:
  10.1 79.4 all-gather.7
  142.3 86.8 all-gather.13
  231.8 74.7 all-gather.9
  309.2 75.1 all-gather.11
  388.2 23.5 reduce-scatter.3
where the time goes:
time: 422 us; the launch traced here: 420 us
  blocking collectives  158 us (37%)
  waiting for transfers between devices  142 us (34%)
  other arithmetic  79 us (19%)
  matrix products  14.9 us (4%)
  between operations  14.6 us (3%)
  local copies, waits for them, and re-layouts  7.21 us (2%)
    select_n x64, other arithmetic, turn(): return jax.tree.map(lambda a, b: jnp.where(reached, a, b), new, before)  67.4 us
    all_gather x1, waiting for transfers between devices, on_device(): lax.all_gather(out_weight, 'seq', axis=1, tiled=True)  64.6 us
    all_gather x1, blocking collectives, on_device(): lax.all_gather(stored[2], 'seq', axis=0, tiled=True)  48.3 us
    all_gather x1, blocking collectives, on_device(): lax.all_gather(stored[3], 'seq', axis=0, tiled=True)  46.7 us
    all_gather x1, waiting for transfers between devices, prefix_2(): lax.all_gather(part.astype(kind), axis)  43.4 us
    all_gather x1, blocking collectives, prefix_2(): lax.all_gather(part.astype(kind), axis)  38.1 us
    unnamed x6, waiting for transfers between devices  23.8 us
    all_gather x1, blocking collectives, on_device(): gathered = lax.all_gather(hidden_in, 'tp', axis=1, tiled=True)  14.2 us
  transfers between devices with their start and end apart: 6, of which 5 were waited for; matrix products, arithmetic and copies ran while one was open for 21% of the time, Pallas kernels for 0%

commit v1 on v0

--- a/solution.py
+++ b/solution.py
@@ -158,7 +158,7 @@
         gate_all.astype(jnp.float32)
     )
     squares = jnp.sum(gated * gated, axis=1)
-    square_total = lax.psum(squares, "tp")
+    square_total = jnp.sum(lax.all_gather(squares, "tp"), axis=0)
     mean_square = square_total / (local_inner * lax.axis_size("tp"))
     normed = (gated * lax.rsqrt(mean_square + EPSILON)[:, None] * norm_gain[None, :]).astype(
         jnp.bfloat16

time: 422 us -> 422 us (level)
    psum x1 -> x0, blocking collectives: 10.5 us -> none  [on_device(): square_total = lax.psum(squares, 'tp')]
    all_gather x0 -> x1, blocking collectives: none -> 9.71 us  [on_device(): square_total = jnp.sum(lax.all_gather(squares, 'tp'), axis=0)]
where the time goes in v1:
time: 422 us; the launch traced here: 420 us
  blocking collectives  157 us (37%)
  waiting for transfers between devices  143 us (34%)
  other arithmetic  79 us (19%)
  matrix products  14.9 us (4%)
  between operations  14.6 us (3%)
  local copies, waits for them, and re-layouts  7.21 us (2%)
    select_n x64, other arithmetic, turn(): return jax.tree.map(lambda a, b: jnp.where(reached, a, b), new, before)  67.4 us
    all_gather x1, waiting for transfers between devices, on_device(): lax.all_gather(out_weight, 'seq', axis=1, tiled=True)  65.3 us
    all_gather x1, blocking collectives, on_device(): lax.all_gather(stored[2], 'seq', axis=0, tiled=True)  48.3 us
    all_gather x1, blocking collectives, on_device(): lax.all_gather(stored[3], 'seq', axis=0, tiled=True)  46.7 us
    all_gather x1, waiting for transfers between devices, prefix_2(): lax.all_gather(part.astype(kind), axis)  43.4 us
    all_gather x1, blocking collectives, prefix_2(): lax.all_gather(part.astype(kind), axis)  38.1 us
    unnamed x6, waiting for transfers between devices  23.8 us
    all_gather x1, blocking collectives, on_device(): gathered = lax.all_gather(hidden_in, 'tp', axis=1, tiled=True)  14.2 us
  transfers between devices with their start and end apart: 6, of which 5 were waited for; matrix products, arithmetic and copies ran while one was open for 21% of the time, Pallas kernels for 0%

profile of v1, /device:TPU:2, one launch (start us, length us, event | category | flops | bytes accessed | tf_op | source)
XLA Modules:
  0.0 420.0 jit_solution(11364080849285243726)
XLA Ops:
  6.5 1.5 convert_element_type.112
  13.0 46.7 %all-gather.2 = bf16[64,24,12]{1,2,0:T(8,128)(2,1)S(1)} all-gather(bf16[1,24,12]{1,2,0:T(8,128)(2,1)S(1)} %convert_bitcast_fusion), channel_id=1, replica_groups=mesh['seq'=64,'tp'=4] {'seq'}, dimensions={0}, use_global_device_ids=true | all-gather | bytes 37440 | tf_op jit(solution)/shard_map/all_gather | solution.py:101
  61.4 14.2 %all_gather.34 = bf16[256,1536]{0,1:T(8,128)(2,1)S(1)} all-gather(bf16[256,384]{0,1:T(8,128)(2,1)S(1)} %copy.39), channel_id=1, replica_groups=mesh['seq'=64,'tp'=4] {'tp'}, dimensions={1}, use_global_device_ids=true | all-gather | bytes 983040 | tf_op jit(solution)/shard_map/all_gather | solution.py:85
  80.0 48.3 %all_gather.36 = bf16[1536,256]{1,0:T(8,128)(2,1)S(1)} all-gather(bf16[24,256]{1,0:T(8,128)(2,1)S(1)} %convert_element_type.114), channel_id=1, replica_groups=mesh['seq'=64,'tp'=4] {'seq'}, dimensions={0}, use_global_device_ids=true | all-gather | bytes 798720 | tf_op jit(solution)/shard_map/all_gather | solution.py:100
  128.3 1.3 broadcast_compare_fusion
  130.1 2.5 convolution_convert_fusion.2
  132.6 2.3 collective-permute-start
  134.9 4.8 %collective-permute-done = bf16[3,1024]{1,0:T(4,128)(2,1)S(1)} collective-permute-done((bf16[3,1024]{1,0:T(4,128)(2,1)S(1)}, bf16[3,1024]{1,0:T(4,128)(2,1)S(1)}, u32[]{:S(2)}, u32[]{:S(2)}) %collective-permute-start) | collective-permute-done | bytes 6176 | tf_op jit(solution)/shard_map/ppermute | solution.py:13
  140.9 1.2 fusion.20
  143.9 38.1 %all-gather.3 = bf16[64,1,12]{2,1,0:T(2,128)(2,1)S(1)} all-gather(bf16[1,1,12]{2,1,0:T(2,128)(2,1)S(1)} %bitcast.97), channel_id=1, replica_groups=mesh['seq'=64,'tp'=4] {'seq'}, dimensions={0}, use_global_device_ids=true | all-gather | bytes 1560 | tf_op jit(solution)/shard_map/all_gather | solution.py:19
  182.2 3.6 fusion.14
  185.8 43.4 %all-gather.16.cloned.1.call-done = bf16[768,64,128]{2,1,0:T(8,128)(2,1)} async-done(((bf16[12,64,128]{2,1,0:T(8,128)(2,1)}), bf16[768,64,128]{2,1,0:T(8,128)(2,1)}) %all-gather.16.cloned.1.call-update) | async-done | bytes 12582928 | tf_op jit(solution)/shard_map/all_gather | solution.py:19
  229.1 70.1 %while.14 = (s32[]{:T(128)}, f32[12,64,128]{2,1,0:T(8,128)S(1)}, s32[]{:T(128)}, bf16[64,12]{1,0:T(8,128)(2,1)S(1)}, bf16[64,12,64,128]{3,2,1,0:T(8,128)(2,1)}, /*index=5*/s32[]{:T(128)}, s32[]{:T(128)}) while((s32[]{:T(128)}, f32[12,64,128]{2,1,0:T(8,128)S(1)}, s32[]{:T(128)}, bf16[64,12]{1,0:T(8,128)(2,1)S(1)}, ...), condition=%wide.region_7.8_spmd.clone, body=%wide.region_6.7_spmd.clone.sunk | while | flops 491536 | bytes 983265 | solution.py:32
  278.4 1.1 fusion.58
  283.9 1.1 fusion.58
  299.3 1.6 fusion.18
  301.2 5.5 %all-gather.12.cloned.1.call-done = bf16[1536,768]{1,0:T(8,128)(2,1)} async-done(((bf16[24,768]{1,0:T(8,128)(2,1)}), bf16[1536,768]{1,0:T(8,128)(2,1)}) %all-gather.12.cloned.1.call-update) | async-done | bytes 2359312 | tf_op jit(solution)/shard_map/all_gather | solution.py:98
  306.7 2.7 multiply_reduce_fusion
  309.4 9.7 %all-gather.4 = f32[4,1,256]{2,1,0:T(1,128)S(1)} all-gather(f32[1,1,256]{2,1,0:T(1,128)S(1)} %bitcast.98), channel_id=3, replica_groups=mesh['seq'=64,'tp'=4] {'tp'}, dimensions={0}, use_global_device_ids=true | all-gather | bytes 5120 | tf_op jit(solution)/shard_map/all_gather | solution.py:161
  319.1 65.3 %all-gather.14.cloned.1.call-done = bf16[768,1536]{0,1:T(8,128)(2,1)} async-done(((bf16[768,24]{0,1:T(8,128)(2,1)}), bf16[768,1536]{0,1:T(8,128)(2,1)}) %all-gather.14.cloned.1.call-update) | async-done | bytes 2359312 | tf_op jit(solution)/shard_map/all_gather | solution.py:169
  384.4 2.5 convolution_convert_fusion
  386.9 1.2 copy.50
  388.1 23.7 %reduce-scatter.4.cloned.1.call-done = bf16[384,256]{1,0:T(8,128)(2,1)} async-done(((bf16[1536,256]{1,0:T(8,128)(2,1)}), bf16[384,256]{1,0:T(8,128)(2,1)}) %reduce-scatter.4.cloned.1.call-update) | async-done | bytes 196624
  411.8 1.7 copy.51
  (205 shorter events, 79.5 us)
Async XLA Ops:
  6.5 123.6 %all-gather.10.cloned.1.call-start = ((), (), s32[]{:S(2)}) async-start(), calls=%async_computation.1 | async-start | bytes 2396160 | tf_op jit(solution)/shard_map/all_gather | solution.py:99
  8.1 221.1 %all-gather.16.cloned.1.call-start = ((), (), s32[]{:S(2)}) async-start(), calls=%async_computation.4 | async-start | bytes 12779520 | tf_op jit(solution)/shard_map/all_gather | solution.py:19
  75.6 0.9 copy-start.5
  76.2 3.6 copy-start.2
  76.2 3.6 copy-start.4
  132.6 7.1 %collective-permute-start = (bf16[3,1024]{1,0:T(4,128)(2,1)S(1)}, bf16[3,1024]{1,0:T(4,128)(2,1)S(1)}, u32[]{:S(2)}, u32[]{:S(2)}) collective-permute-start(bf16[3,1024]{1,0:T(4,128)(2,1)S(1)} %fusion.40), channel_id=1, source_target_pairs={{0,4},{4,8},{8,12},{12,16},{16,20},{20,24},{24,28},{28,32},{32,36}... | collective-permute-start | bytes 18440 | tf_op jit(solution)/shard_map/ppermute | solution.py:13
  139.9 2.3 copy-start
  139.9 3.1 copy-start.1
  142.2 164.5 %all-gather.12.cloned.1.call-start = ((), (), s32[]{:S(2)}) async-start(), calls=%async_computation.2 | async-start | bytes 2396160 | tf_op jit(solution)/shard_map/all_gather | solution.py:98
  142.9 241.5 %all-gather.14.cloned.1.call-start = ((), (), s32[]{:S(2)}) async-start(), calls=%async_computation.3 | async-start | bytes 2396160 | tf_op jit(solution)/shard_map/all_gather | solution.py:169
  143.6 268.2 %reduce-scatter.4.cloned.1.call-start = ((), (), s32[]{:S(2)}) async-start(), calls=%async_computation.5 | async-start | bytes 983040
  229.1 70.1 %copy-start.6 = (f32[12]{0:T(128)S(1)}, f32[12]{0:T(128)}, u32[]{:S(2)}) copy-start(f32[12]{0:T(128)} %param.25) | copy-start | bytes 148
  301.2 83.2 %copy-start.3 = (f32[768]{0:T(1024)S(1)}, f32[768]{0:T(1024)}, u32[]{:S(2)}) copy-start(f32[768]{0:T(1024)} %param.26) | copy-start | bytes 9220
Sparse Core Ops, SparseCore 0:
  10.1 79.4 all-gather.9
  142.3 86.8 all-gather.15
  231.8 74.7 all-gather.11
  309.2 75.1 all-gather.13
  388.2 23.5 reduce-scatter.3
